TPU v7x, 32 devices: a whole 2x2x4 slice. The times are simulated.
32 devices in a mesh: lat: 4 (over y, x), lon: 8 (over z, core).
Axes of the slice: x: 2, y: 2, z: 4, core: 2. Of those that a mesh axis runs over, the one named last changes fastest.
Arguments:
- fine_map: bfloat16 [4, 48, 256, 400], P(None, 'lat', 'lon'), may hold values from -26 to 26
- ocean_mask: int32 [4, 48, 256], P(None, 'lat', 'lon'), may hold values from 0 to 1
- out_grad: bfloat16 [4, 48, 256, 400], P(None, 'lat', 'lon'), may hold values from -6 to 6
- encode_depth: bfloat16 [7, 7, 400], replicated, may hold values from -0.875 to 0.875
- encode_gain: bfloat16 [400], replicated, may hold values from 0.099609375 to 1.8984375
- encode_shift: bfloat16 [400], replicated, may hold values from -3 to 3
- encode_up: bfloat16 [400, 1600], P('lat'), may hold values from -0.3125 to 0.3125
- encode_up_bias: bfloat16 [1600], replicated, may hold values from -3 to 3
- encode_down: bfloat16 [1600, 400], P('lat'), may hold values from -0.15625 to 0.15625
- encode_down_bias: bfloat16 [400], replicated, may hold values from -3 to 3
- widen_weight: bfloat16 [400, 800], P('lat'), may hold values from -0.3125 to 0.3125
- widen_bias: bfloat16 [800], replicated, may hold values from -3 to 3
- bottle_depth: bfloat16 [7, 7, 800], replicated, may hold values from -0.875 to 0.875
- bottle_gain: bfloat16 [800], replicated, may hold values from 0.099609375 to 1.8984375
- bottle_shift: bfloat16 [800], replicated, may hold values from -3 to 3
- bottle_up: bfloat16 [800, 3200], P('lat'), may hold values from -0.21875 to 0.21875
- bottle_up_bias: bfloat16 [3200], replicated, may hold values from -3 to 3
- bottle_down: bfloat16 [3200, 800], P('lat'), may hold values from -0.109375 to 0.109375
- bottle_down_bias: bfloat16 [800], replicated, may hold values from -3 to 3
- merge_weight: bfloat16 [1200, 400], P('lat'), may hold values from -0.1875 to 0.1875
- merge_bias: bfloat16 [400], replicated, may hold values from -3 to 3
- decode_depth: bfloat16 [7, 7, 400], replicated, may hold values from -0.875 to 0.875
- decode_gain: bfloat16 [400], replicated, may hold values from 0.099609375 to 1.8984375
- decode_shift: bfloat16 [400], replicated, may hold values from -3 to 3
- decode_up: bfloat16 [400, 1600], P('lat'), may hold values from -0.3125 to 0.3125
- decode_up_bias: bfloat16 [1600], replicated, may hold values from -3 to 3
- decode_down: bfloat16 [1600, 400], P('lat'), may hold values from -0.15625 to 0.15625
- decode_down_bias: bfloat16 [400], replicated, may hold values from -3 to 3
Outputs:
- result: bfloat16 [4, 48, 256, 400], P(None, 'lat', 'lon')
- fine_grad: bfloat16 [4, 48, 256, 400], P(None, 'lat', 'lon')
- encode_depth_grad: float32 [7, 7, 400], replicated
- encode_gain_grad: float32 [400], replicated
- encode_shift_grad: float32 [400], replicated
- encode_up_grad: float32 [400, 1600], replicated
- encode_up_bias_grad: float32 [1600], replicated
- encode_down_grad: float32 [1600, 400], replicated
- encode_down_bias_grad: float32 [400], replicated
- widen_weight_grad: float32 [400, 800], replicated
- widen_bias_grad: float32 [800], replicated
- bottle_depth_grad: float32 [7, 7, 800], replicated
- bottle_gain_grad: float32 [800], replicated
- bottle_shift_grad: float32 [800], replicated
- bottle_up_grad: float32 [800, 3200], replicated
- bottle_up_bias_grad: float32 [3200], replicated
- bottle_down_grad: float32 [3200, 800], replicated
- bottle_down_bias_grad: float32 [800], replicated
- merge_weight_grad: float32 [1200, 400], replicated
- merge_bias_grad: float32 [400], replicated
- decode_depth_grad: float32 [7, 7, 400], replicated
- decode_gain_grad: float32 [400], replicated
- decode_shift_grad: float32 [400], replicated
- decode_up_grad: float32 [400, 1600], replicated
- decode_up_bias_grad: float32 [1600], replicated
- decode_down_grad: float32 [1600, 400], replicated
- decode_down_bias_grad: float32 [400], replicated
All inputs are finite; a program needn't handle non-finite values.
Results may differ from a plain program's by a relative error of at most 0.018.
Values may be sent and summed in bfloat16 or wider, within the bound.
No kernel may reach another device: no remote copies, remote signals or barrier semaphores. Data moves between devices by JAX's collectives and lax.ppermute only.
A program may use at most 320 MiB of HBM per device.

v0:
```python
import math
import jax
import jax.numpy as jnp
from jax import lax
from jax.sharding import PartitionSpec as P

epsilon = 1e-05


def padded(block, sides, width, periodic):
    for axis, dim in sides:
        count = lax.axis_size(axis)
        forward = [(i, i + 1) for i in range(count - 1)]
        if periodic:
            forward.append((count - 1, 0))
        backward = [(target, source) for source, target in forward]
        low = lax.ppermute(
            lax.slice_in_dim(block, block.shape[dim] - width, None, axis=dim), axis, forward
        )
        high = lax.ppermute(lax.slice_in_dim(block, 0, width, axis=dim), axis, backward)
        block = jnp.concatenate([low, block, high], axis=dim)
    return block


def widen_map(source):
    wrapped = padded(source, (("lon", 2),), 3, True)
    return padded(wrapped, (("lat", 1),), 3, False)


def stencil(extended, kernel, height, breadth):
    taps = kernel.astype(jnp.float32)
    summed = jnp.zeros((extended.shape[0], height, breadth, extended.shape[3]), jnp.float32)
    for across in range(7):
        for column in range(7):
            summed = summed + taps[across, column] * extended[
                :, across : across + height, column : column + breadth, :
            ].astype(jnp.float32)
    return summed


def kernel_terms(extended, grad_mixed, height, breadth):
    upstream = grad_mixed.astype(jnp.float32)
    all_rows = []
    for across in range(7):
        row_terms = []
        for column in range(7):
            window = extended[:, across : across + height, column : column + breadth, :].astype(
                jnp.float32
            )
            row_terms.append(jnp.sum(window * upstream, axis=(0, 1, 2)))
        all_rows.append(jnp.stack(row_terms))
    return jnp.stack(all_rows)


def cross_rows(former, latter):
    return lax.dot_general(
        former, latter, (((0,), (0,)), ((), ())), preferred_element_type=jnp.float32
    )


def by_transpose(former, latter):
    return lax.dot_general(
        former, latter, (((1,), (1,)), ((), ())), preferred_element_type=jnp.float32
    )


def exact_gelu(values):
    return jax.nn.gelu(values, approximate=False)


def block_forward(source, params, sea_mask):
    kernel, scale_gain, norm_shift, up_weight, up_bias, down_weight, down_bias = params
    date_count, height, breadth, channels = source.shape
    extended = widen_map(source)
    mixed = stencil(extended, kernel, height, breadth)
    local_sums = (
        jnp.sum(sea_mask * mixed, axis=(0, 1, 2)),
        jnp.sum(sea_mask * mixed * mixed, axis=(0, 1, 2)),
        jnp.sum(sea_mask),
    )
    first_sum, square_sum, ocean_count = lax.psum(
        (local_sums[0], local_sums[1], local_sums[2]), ("lat", "lon")
    )
    mean_value = first_sum / ocean_count
    norm_factor = lax.rsqrt(square_sum / ocean_count - mean_value * mean_value + epsilon)
    unit_norm = (mixed - mean_value) * norm_factor
    normed = (
        (unit_norm * scale_gain.astype(jnp.float32) + norm_shift.astype(jnp.float32))
        .astype(jnp.bfloat16)
        .reshape(-1, channels)
    )
    hidden = jnp.dot(normed, up_weight, preferred_element_type=jnp.float32) + up_bias.astype(
        jnp.float32
    )
    active = exact_gelu(hidden).astype(jnp.bfloat16)
    branch = jnp.dot(active, down_weight, preferred_element_type=jnp.float32) + down_bias.astype(
        jnp.float32
    )
    output = sea_mask * (source.astype(jnp.float32) + branch.reshape(source.shape))
    stored = (extended, unit_norm, norm_factor, ocean_count, normed, hidden, active)
    return (output, stored)


def block_backward(grad_output, params, sea_mask, stored):
    kernel, scale_gain, norm_shift, up_weight, up_bias, down_weight, down_bias = params
    extended, unit_norm, norm_factor, ocean_count, normed, hidden_store, active = stored
    date_count, height, breadth, channels = unit_norm.shape
    grad_branch = (sea_mask * grad_output).astype(jnp.bfloat16).reshape(-1, channels)
    grad_down = cross_rows(active, grad_branch)
    grad_down_bias = jnp.sum(grad_branch.astype(jnp.float32), axis=0)
    grad_active = by_transpose(grad_branch, down_weight)
    unused_value, gelu_back = jax.vjp(exact_gelu, hidden_store)
    grad_hidden = gelu_back(grad_active)[0].astype(jnp.bfloat16)
    grad_up = cross_rows(normed, grad_hidden)
    grad_up_bias = jnp.sum(grad_hidden.astype(jnp.float32), axis=0)
    grad_normed = by_transpose(grad_hidden, up_weight).reshape(unit_norm.shape)
    local_back = (
        jnp.sum(grad_normed, axis=(0, 1, 2)),
        jnp.sum(grad_normed * unit_norm, axis=(0, 1, 2)),
    )
    grad_shift, grad_gain = lax.psum((local_back[0], local_back[1]), ("lat", "lon"))
    gain_float = scale_gain.astype(jnp.float32)
    grad_mixed = norm_factor * (
        gain_float * grad_normed
        - sea_mask / ocean_count * (gain_float * grad_shift + unit_norm * (gain_float * grad_gain))
    )
    grad_mixed = grad_mixed.astype(jnp.bfloat16)
    grad_extended = widen_map(grad_mixed)
    grad_source = sea_mask * grad_output + stencil(
        grad_extended, kernel[::-1, ::-1], height, breadth
    )
    grad_kernel = kernel_terms(extended, grad_mixed, height, breadth)
    return (
        grad_source,
        (grad_kernel, grad_gain, grad_shift, grad_up, grad_up_bias, grad_down, grad_down_bias),
    )


def unpack(vector, extents):
    pieces = []
    offset = 0
    for extent in extents:
        length = math.prod(extent)
        pieces.append(vector[offset : offset + length].reshape(extent))
        offset = offset + length
    return pieces


def shards(
    fine_map,
    ocean_mask,
    out_grad,
    encode_depth,
    encode_gain,
    encode_shift,
    encode_up,
    encode_up_bias,
    encode_down,
    encode_down_bias,
    widen_weight,
    widen_bias,
    bottle_depth,
    bottle_gain,
    bottle_shift,
    bottle_up,
    bottle_up_bias,
    bottle_down,
    bottle_down_bias,
    merge_weight,
    merge_bias,
    decode_depth,
    decode_gain,
    decode_shift,
    decode_up,
    decode_up_bias,
    decode_down,
    decode_down_bias,
):
    (
        encode_up,
        encode_down,
        widen_weight,
        bottle_up,
        bottle_down,
        merge_weight,
        decode_up,
        decode_down,
    ) = (
        lax.all_gather(encode_up, "lat", axis=0, tiled=True),
        lax.all_gather(encode_down, "lat", axis=0, tiled=True),
        lax.all_gather(widen_weight, "lat", axis=0, tiled=True),
        lax.all_gather(bottle_up, "lat", axis=0, tiled=True),
        lax.all_gather(bottle_down, "lat", axis=0, tiled=True),
        lax.all_gather(merge_weight, "lat", axis=0, tiled=True),
        lax.all_gather(decode_up, "lat", axis=0, tiled=True),
        lax.all_gather(decode_down, "lat", axis=0, tiled=True),
    )
    date_count, height, breadth, channels = fine_map.shape
    half_height, half_breadth = (height // 2, breadth // 2)
    wide_channels = widen_weight.shape[1]
    sea_fine = ocean_mask.astype(jnp.float32)[..., None]
    sea_coarse = jnp.max(
        sea_fine.reshape(date_count, half_height, 2, half_breadth, 2, 1), axis=(2, 4)
    )
    encode = (
        encode_depth,
        encode_gain,
        encode_shift,
        encode_up,
        encode_up_bias,
        encode_down,
        encode_down_bias,
    )
    bottle = (
        bottle_depth,
        bottle_gain,
        bottle_shift,
        bottle_up,
        bottle_up_bias,
        bottle_down,
        bottle_down_bias,
    )
    decode = (
        decode_depth,
        decode_gain,
        decode_shift,
        decode_up,
        decode_up_bias,
        decode_down,
        decode_down_bias,
    )
    merge_upper = merge_weight[:wide_channels]
    merge_lower = merge_weight[wide_channels:]
    encode_out, encode_stored = block_forward(fine_map, encode, sea_fine)
    skip_map = encode_out.astype(jnp.bfloat16)
    skip_rows = skip_map.reshape(-1, channels)
    blocks_fine = skip_map.reshape(date_count, half_height, 2, half_breadth, 2, channels).astype(
        jnp.float32
    )
    pooled = (jnp.sum(blocks_fine, axis=(2, 4)) * 0.25).astype(jnp.bfloat16).reshape(-1, channels)
    coarse_in = jnp.dot(
        pooled, widen_weight, preferred_element_type=jnp.float32
    ) + widen_bias.astype(jnp.float32)
    coarse_in = coarse_in.astype(jnp.bfloat16).reshape(
        date_count, half_height, half_breadth, wide_channels
    )
    coarse_out, coarse_stored = block_forward(coarse_in, bottle, sea_coarse)
    coarse_low = coarse_out.astype(jnp.bfloat16).reshape(-1, wide_channels)
    upper_part = jnp.dot(coarse_low, merge_upper, preferred_element_type=jnp.float32)
    upper_part = upper_part.reshape(date_count, half_height, 1, half_breadth, 1, channels)
    lower_part = jnp.dot(skip_rows, merge_lower, preferred_element_type=jnp.float32)
    lower_part = lower_part.reshape(date_count, half_height, 2, half_breadth, 2, channels)
    merged = (lower_part + upper_part).reshape(
        date_count, height, breadth, channels
    ) + merge_bias.astype(jnp.float32)
    decode_in = merged.astype(jnp.bfloat16)
    decode_out, decode_stored = block_forward(decode_in, decode, sea_fine)
    result = decode_out.astype(jnp.bfloat16)
    grad_decode_in, decode_grads = block_backward(
        out_grad.astype(jnp.float32), decode, sea_fine, decode_stored
    )
    grad_merged = grad_decode_in.astype(jnp.bfloat16).reshape(-1, channels)
    coarse_grid = coarse_low.reshape(date_count, half_height, 1, half_breadth, 1, wide_channels)
    upsampled_rows = jnp.broadcast_to(
        coarse_grid, (date_count, half_height, 2, half_breadth, 2, wide_channels)
    ).reshape(-1, wide_channels)
    grad_merge_weight = jnp.concatenate(
        [cross_rows(upsampled_rows, grad_merged), cross_rows(skip_rows, grad_merged)], axis=0
    )
    grad_merge_bias = jnp.sum(grad_merged.astype(jnp.float32), axis=0)
    grad_upsampled = by_transpose(grad_merged, merge_upper)
    grad_coarse = jnp.sum(
        grad_upsampled.reshape(date_count, half_height, 2, half_breadth, 2, wide_channels),
        axis=(2, 4),
    )
    grad_skip_direct = by_transpose(grad_merged, merge_lower)
    grad_coarse_in, bottle_grads = block_backward(grad_coarse, bottle, sea_coarse, coarse_stored)
    grad_wide = grad_coarse_in.astype(jnp.bfloat16).reshape(-1, wide_channels)
    grad_widen_weight = cross_rows(pooled, grad_wide)
    grad_widen_bias = jnp.sum(grad_wide.astype(jnp.float32), axis=0)
    grad_pooled = (
        by_transpose(grad_wide, widen_weight).reshape(
            date_count, half_height, 1, half_breadth, 1, channels
        )
        * 0.25
    )
    grad_skip = (
        grad_skip_direct.reshape(date_count, half_height, 2, half_breadth, 2, channels)
        + grad_pooled
    )
    grad_skip = grad_skip.reshape(date_count, height, breadth, channels)
    grad_fine, encode_grads = block_backward(grad_skip, encode, sea_fine, encode_stored)
    fine_grad = grad_fine.astype(jnp.bfloat16)
    large_parts = [
        encode_grads[3],
        encode_grads[5],
        grad_widen_weight,
        bottle_grads[3],
        bottle_grads[5],
        grad_merge_weight,
        decode_grads[3],
        decode_grads[5],
    ]
    large_extents = [part_grad.shape for part_grad in large_parts]
    large_vector = jnp.concatenate([part_grad.reshape(-1) for part_grad in large_parts])
    share = lax.psum_scatter(large_vector, ("lat", "lon"), scatter_dimension=0, tiled=True)
    large_total = lax.all_gather(
        share.astype(jnp.bfloat16), ("lat", "lon"), axis=0, tiled=True
    ).astype(share.dtype)
    small_parts = [
        encode_grads[0],
        encode_grads[4],
        encode_grads[6],
        grad_widen_bias,
        bottle_grads[0],
        bottle_grads[4],
        bottle_grads[6],
        grad_merge_bias,
        decode_grads[0],
        decode_grads[4],
        decode_grads[6],
    ]
    small_extents = [part_grad.shape for part_grad in small_parts]
    small_vector = jnp.concatenate([part_grad.reshape(-1) for part_grad in small_parts])
    small_total = lax.psum(small_vector, ("lat", "lon"))
    (
        encode_up_sum,
        encode_down_sum,
        widen_w_sum,
        bottle_up_sum,
        bottle_down_sum,
        merge_w_sum,
        decode_up_sum,
        decode_down_sum,
    ) = unpack(large_total, large_extents)
    (
        encode_kernel_sum,
        encode_upb_sum,
        encode_downb_sum,
        widen_b_sum,
        bottle_kernel_sum,
        bottle_upb_sum,
        bottle_downb_sum,
        merge_b_sum,
        decode_kernel_sum,
        decode_upb_sum,
        decode_downb_sum,
    ) = unpack(small_total, small_extents)
    return (
        result,
        fine_grad,
        encode_kernel_sum,
        encode_grads[1],
        encode_grads[2],
        encode_up_sum,
        encode_upb_sum,
        encode_down_sum,
        encode_downb_sum,
        widen_w_sum,
        widen_b_sum,
        bottle_kernel_sum,
        bottle_grads[1],
        bottle_grads[2],
        bottle_up_sum,
        bottle_upb_sum,
        bottle_down_sum,
        bottle_downb_sum,
        merge_w_sum,
        merge_b_sum,
        decode_kernel_sum,
        decode_grads[1],
        decode_grads[2],
        decode_up_sum,
        decode_upb_sum,
        decode_down_sum,
        decode_downb_sum,
    )


def solution(mesh):
    placed = (
        P(None, "lat", "lon", None),
        P(None, "lat", "lon"),
        P(None, "lat", "lon", None),
        P(),
        P(),
        P(),
        P("lat", None),
        P(),
        P("lat", None),
        P(),
        P("lat", None),
        P(),
        P(),
        P(),
        P(),
        P("lat", None),
        P(),
        P("lat", None),
        P(),
        P("lat", None),
        P(),
        P(),
        P(),
        P(),
        P("lat", None),
        P(),
        P("lat", None),
        P(),
    )
    return jax.shard_map(
        shards,
        mesh=mesh,
        in_specs=placed,
        out_specs=(
            P(None, "lat", "lon", None),
            P(None, "lat", "lon", None),
            P(),
            P(),
            P(),
            P(),
            P(),
            P(),
            P(),
            P(),
            P(),
            P(),
            P(),
            P(),
            P(),
            P(),
            P(),
            P(),
            P(),
            P(),
            P(),
            P(),
            P(),
            P(),
            P(),
            P(),
            P(),
        ),
        check_vma=False,
    )
```

profile of v0, /device:TPU:0, one launch (start us, length us, event | category | flops | bytes accessed | tf_op | source)
XLA Modules:
  0.0 2301.6 jit_solution(13207212915180531190)
XLA Ops:
  32.2 21.0 all-gather.1
  53.2 15.3 all-gather.2
  125.6 26.5 %multiply_reduce_fusion.1 = (f32[400]{0:T(512)}, f32[400]{0:T(512)}, f32[4,12,32,400]{3,2,1,0:T(8,128)}) fusion(f32[4,12,32]{2,1,0:T(8,128)S(1)} %copy-done.50, bf16[4,15,38,400]{3,2,1,0:T(8,128)(2,1)S(1)} %get-tuple-element.441, f32[400]{0:T(512)} %bitcast.523, f32[400]{0:T(512)} %bitcast.522, f32[400]{0:T(512)} %bitcast.521, f32[400]{0:T(512)} %bitcast.520, ...), kind=kLoop, calls=%fused_computation.214 | loop fusion | flops 97688800 | bytes 59185344 | tf_op jit(solution)/shard_map/reduce_sum | solution.py:77
  152.1 43.1 %all-reduce.7 = (f32[400]{0:T(512)S(1)}, f32[]{:T(128)}, f32[400]{0:T(512)S(1)}) all-reduce(f32[400]{0:T(512)} %get-tuple-element.207, f32[]{:T(128)} %convert_reduce_fusion.9, f32[400]{0:T(512)} %get-tuple-element.206), channel_id=1, replica_groups=mesh['lat'=4,'lon'=8] {'lat','lon'}, use_global_device_ids=true, to_apply=%region_5.0 | all-reduce | flops 801 | bytes 6408 | tf_op jit(solution)/shard_map/psum | solution.py:81
  201.4 29.4 %multiply_convert_fusion.1 = (bf16[1536,1600]{0,1:T(8,128)(2,1)}, f32[1536,1600]{0,1:T(8,128)}, f32[1536,1600]{0,1:T(8,128)}) fusion(f32[1600]{0:T(1024)S(1)} %copy-done.321, bf16[1536,400]{1,0:T(8,128)(2,1)S(1)} %bitcast.461, bf16[400,1600]{1,0:T(8,128)(2,1)} %reshape.643), kind=kOutput, calls=%fused_computation.171 | convolution fusion | flops 2128281600 | bytes 27091200 | tf_op jit(solution)/shard_map/dot_general | solution.py:92
  269.2 12.5 collective-permute-done.6
  281.7 18.0 collective-permute-done.7
  313.0 39.1 %all-reduce.6 = (f32[800]{0:T(1024)S(1)}, f32[]{:T(128)}, f32[800]{0:T(1024)S(1)}) all-reduce(f32[800]{0:T(1024)S(1)} %get-tuple-element.279, f32[]{:T(128)} %reduce_sum.1550, f32[800]{0:T(1024)S(1)} %get-tuple-element.278), channel_id=1, replica_groups=mesh['lat'=4,'lon'=8] {'lat','lon'}, use_global_device_ids=true, to_apply=%region_13.0 | all-reduce | flops 1601 | bytes 12808 | tf_op jit(solution)/shard_map/psum | solution.py:81
  353.1 16.4 multiply_convert_fusion.2
  407.7 12.8 collective-permute-done.11
  425.0 24.8 %multiply_reduce_fusion = (f32[400]{0:T(512)S(1)}, f32[400]{0:T(512)S(1)}, f32[4,12,32,400]{3,2,1,0:T(8,128)}) fusion(f32[4,12,32]{2,1,0:T(8,128)S(1)} %copy-done.52, bf16[4,15,38,400]{3,2,1,0:T(8,128)(2,1)S(1)} %get-tuple-element.437, f32[400]{0:T(512)} %bitcast.594, f32[400]{0:T(512)} %bitcast.593, f32[400]{0:T(512)} %bitcast.592, f32[400]{0:T(512)} %bitcast.591, ...), kind=kLoop, calls=%fused_computation.212 | loop fusion | flops 103218400 | bytes 55614144 | tf_op jit(solution)/shard_map/reduce_sum | solution.py:77
  449.9 38.6 %all-reduce.5 = (f32[400]{0:T(512)S(1)}, f32[400]{0:T(512)S(1)}) all-reduce(f32[400]{0:T(512)S(1)} %get-tuple-element.205, f32[400]{0:T(512)S(1)} %get-tuple-element.204), channel_id=1, replica_groups=mesh['lat'=4,'lon'=8] {'lat','lon'}, use_global_device_ids=true, to_apply=%region_17.0 | all-reduce | flops 800 | bytes 6400 | tf_op jit(solution)/shard_map/psum | solution.py:81
  492.8 30.1 %multiply_convert_fusion = (bf16[1536,1600]{0,1:T(8,128)(2,1)}, f32[1536,1600]{0,1:T(8,128)}, f32[1536,1600]{0,1:T(8,128)}) fusion(f32[1600]{0:T(1024)S(1)} %copy-done.320, bf16[1536,400]{1,0:T(8,128)(2,1)S(1)} %bitcast.463, bf16[400,1600]{1,0:T(8,128)(2,1)S(1)} %copy-done.62), kind=kOutput, calls=%fused_computation.158 | convolution fusion | flops 2128281600 | bytes 27091200 | tf_op jit(solution)/shard_map/dot_general | solution.py:92
  522.9 12.3 convert_reduce_fusion
  550.6 41.1 %all-reduce.4 = (f32[400]{0:T(512)S(1)}, f32[400]{0:T(512)S(1)}) all-reduce(f32[400]{0:T(512)S(1)} %multiply_reduce_fusion.3, f32[400]{0:T(512)S(1)} %get-tuple-element.689), channel_id=1, replica_groups=mesh['lat'=4,'lon'=8] {'lat','lon'}, use_global_device_ids=true, to_apply=%region_21.0 | all-reduce | flops 800 | bytes 6400 | tf_op jit(solution)/shard_map/psum | solution.py:121
  591.7 23.0 %fusion.193 = (f32[400]{0:T(512)S(1)}, f32[400]{0:T(512)S(1)}, f32[400]{0:T(512)S(1)}, f32[400]{0:T(512)S(1)}, f32[400]{0:T(512)S(1)}, /*index=5*/f32[400]{0:T(5...) fusion(bf16[4,15,38,400]{3,2,1,0:T(8,128)(2,1)} %copy-done.4, ...), kind=kLoop, calls=%fused_computation.486 | loop fusion | flops 39314400 | bytes 28305344 | tf_op jit(solution)/shard_map/reduce_sum | solution.py:50
  654.7 13.3 fusion.192
  681.9 12.6 collective-permute-done.15
  698.5 25.1 %convert_reduce_fusion.4 = (f32[400]{0:T(512)}, bf16[4,12,32,400]{3,2,1,0:T(8,128)(2,1)S(1)}) fusion(bf16[4,15,38,400]{3,2,1,0:T(8,128)(2,1)S(1)} %get-tuple-element.433, f32[400]{0:T(512)S(1)} %bitcast.605, f32[400]{0:T(512)S(1)} %bitcast.604, f32[400]{0:T(512)S(1)} %bitcast.603, f32[400]{0:T(512)S(1)} %bitcast.602, f32[400]{0:T(512)S(1)} %bitcast.601, ...), kind=kLoop, calls=%fused_computation.567 | loop fusion | flops 104447600 | bytes 55612544 | tf_op jit(solution)/shard_map/reduce_sum | solution.py:270
  764.3 39.1 %all-reduce.3 = (f32[800]{0:T(1024)S(1)}, f32[800]{0:T(1024)S(1)}) all-reduce(f32[800]{0:T(1024)S(1)} %multiply_reduce_fusion.5, f32[800]{0:T(1024)S(1)} %get-tuple-element.691), channel_id=1, replica_groups=mesh['lat'=4,'lon'=8] {'lat','lon'}, use_global_device_ids=true, to_apply=%region_26.0 | all-reduce | flops 1600 | bytes 12800 | tf_op jit(solution)/shard_map/psum | solution.py:121
  863.8 14.2 reshape.631
  957.2 87.2 %dynamic-update-slice.4 = f32[8480000]{0:T(1024)} dynamic-update-slice(f32[8480000]{0:T(1024)} %dynamic-update-slice.3, f32[2560000]{0:T(1024)} %reshape.630, s32[]{} %constant.210) | dynamic-update-slice | bytes 20480004
  1044.4 87.0 %dynamic-update-slice.5 = f32[8480000]{0:T(1024)} dynamic-update-slice(f32[8480000]{0:T(1024)} %dynamic-update-slice.4, f32[2560000]{0:T(1024)} %reshape.631, s32[]{} %constant.211) | dynamic-update-slice | bytes 20480004
  1131.4 17.6 dynamic-update-slice.6
  1149.0 21.8 dynamic-update-slice.7
  1170.7 22.7 dynamic-update-slice.8
  1199.4 553.5 %all-reduce.15 = (bf16[8480000]{0:T(1024)(128)(2,1)}, f32[400]{0:T(512)S(1)}, f32[400]{0:T(512)S(1)}) all-reduce(f32[8480000]{0:T(1024)} %dynamic-update-slice.8, f32[400]{0:T(512)S(1)} %multiply_reduce_fusion.2, f32[400]{0:T(512)S(1)} %get-tuple-element.693), channel_id=2, replica_groups=mesh['lat'=4,'lon'=8] {'lat','lon'}, use_global_device_ids=true, to_apply=%region_187.0.clone | all-reduce | flops 8480800 | bytes 50886400
  1824.1 94.5 %all-reduce.12.cloned.1.call-done = f32[87600]{0:T(1024)} async-done(((f32[87600]{0:T(1024)}), f32[87600]{0:T(1024)}) %all-reduce.12.cloned.1.call-update) | async-done | bytes 350416 | tf_op jit(solution)/shard_map/psum | solution.py:325
  1932.7 25.4 %fusion.269 = bf16[4,12,32,400]{3,2,1,0:T(8,128)(2,1)} fusion(f32[4,12,32,400]{3,0,2,1:T(4,128)S(1)} %bitcast.451, bf16[4,12,32,400]{3,2,1,0:T(8,128)(2,1)S(1)} %copy-done.17, bf16[4,12,3,400]{3,2,1,0:T(4,128)(2,1)S(1)} %collective-permute-done.21, bf16[4,12,3,400]{3,2,1,0:T(4,128)(2,1)S(1)} %collective-permute-done.20, ...), kind=kLoop, calls=%fused_computation.563 | loop fusion | flops 102604800 | bytes 56839744 | tf_op jit(solution)/shard_map/convert_element_type | solution.py:293
  1958.1 249.6 %all-reduce.14.cloned.1.call-done = bf16[8480000]{0:T(1024)(128)(2,1)} async-done(((bf16[8480000]{0:T(1024)(128)(2,1)}), bf16[8480000]{0:T(1024)(128)(2,1)}) %all-reduce.14.cloned.1.call-update) | async-done | bytes 16960016
  2218.5 13.5 slice.3016
  2232.0 12.2 copy.181
  (1029 shorter events, 588.1 us)
Async XLA Ops:
  7.2 191.1 %all-gather.19.cloned.1.call-start = ((), (), s32[]{:S(2)}) async-start(), calls=%async_computation.6 | async-start | bytes 1730560 | tf_op jit(solution)/shard_map/all_gather | solution.py:189
  8.0 222.9 %all-gather.11.cloned.1.call-start = ((), (), s32[]{:S(2)}) async-start(), calls=%async_computation | async-start | bytes 2048000 | tf_op jit(solution)/shard_map/all_gather | solution.py:190
  8.7 344.4 %all-gather.13.cloned.1.call-start = ((), (), s32[]{:S(2)}) async-start(), calls=%async_computation.1 | async-start | bytes 6400000 | tf_op jit(solution)/shard_map/all_gather | solution.py:192
  9.4 360.1 %all-gather.15.cloned.1.call-start = ((), (), s32[]{:S(2)}) async-start(), calls=%async_computation.2 | async-start | bytes 7168000 | tf_op jit(solution)/shard_map/all_gather | solution.py:193
  10.0 388.8 %all-gather.21.cloned.1.call-start = ((), (), s32[]{:S(2)}) async-start(), calls=%async_computation.7 | async-start | bytes 1730560 | tf_op jit(solution)/shard_map/all_gather | solution.py:195
  10.6 512.3 %all-gather.17.cloned.1.call-start = ((), (), s32[]{:S(2)}) async-start(), calls=%async_computation.3 | async-start | bytes 2048000 | tf_op jit(solution)/shard_map/all_gather | solution.py:196
  11.6 57.0 %collective-permute-start = (bf16[4,12,3,400]{3,2,1,0:T(4,128)(2,1)}, bf16[4,12,3,400]{3,2,1,0:T(4,128)(2,1)}, u32[]{:S(2)}, u32[]{:S(2)}) collective-permute-start(bf16[4,12,3,400]{3,2,1,0:T(4,128)(2,1)} %get-tuple-element.451), channel_id=1, source_target_pairs={{0,1},{1,2},{2,3},{3,4},{4,5},{5,6},{6,7},{7,0},{8,9},{9,10},{10,1... | collective-permute-start | bytes 345608 | tf_op jit(solution)/shard_map/ppermute | solution.py:17
  12.0 56.6 %collective-permute-start.1 = (bf16[4,12,3,400]{3,2,1,0:T(4,128)(2,1)}, bf16[4,12,3,400]{3,2,1,0:T(4,128)(2,1)}, u32[]{:S(2)}, u32[]{:S(2)}) collective-permute-start(bf16[4,12,3,400]{3,2,1,0:T(4,128)(2,1)} %get-tuple-element.452), channel_id=1, source_target_pairs={{1,0},{2,1},{3,2},{4,3},{5,4},{6,5},{7,6},{0,7},{9,8},{10,9},{11,1... | collective-permute-start | bytes 345608 | tf_op jit(solution)/shard_map/ppermute | solution.py:20
  16.1 1902.5 %all-reduce.12.cloned.1.call-start = ((), (), s32[]{:S(2)}) async-start(), calls=%async_computation.4 | async-start | bytes 704512 | tf_op jit(solution)/shard_map/psum | solution.py:325
  70.9 50.0 %collective-permute-start.2 = (bf16[4,3,38,400]{3,2,1,0:T(8,128)(2,1)}, bf16[4,3,38,400]{3,2,1,0:T(8,128)(2,1)}, u32[]{:S(2)}, u32[]{:S(2)}) collective-permute-start(bf16[4,3,38,400]{3,2,1,0:T(8,128)(2,1)} %get-tuple-element.442), channel_id=1, source_target_pairs={{0,8},{8,16},{16,24},{1,9},{9,17},{17,25},{2,10},{10,18},{18,26},{... | collective-permute-start | bytes 1094408 | tf_op jit(solution)/shard_map/ppermute | solution.py:17
  73.8 47.1 %collective-permute-start.3 = (bf16[4,3,38,400]{3,2,1,0:T(8,128)(2,1)}, bf16[4,3,38,400]{3,2,1,0:T(8,128)(2,1)}, u32[]{:S(2)}, u32[]{:S(2)}) collective-permute-start(bf16[4,3,38,400]{3,2,1,0:T(8,128)(2,1)} %get-tuple-element.443), channel_id=1, source_target_pairs={{8,0},{16,8},{24,16},{9,1},{17,9},{25,17},{10,2},{18,10},{26,18},{... | collective-permute-start | bytes 1094408 | tf_op jit(solution)/shard_map/ppermute | solution.py:20
  253.8 7.9 collective-permute-start.4
  253.9 7.8 collective-permute-start.5
  262.8 18.9 collective-permute-start.6
  266.6 33.1 %collective-permute-start.7 = (bf16[4,3,22,800]{3,2,1,0:T(8,128)(2,1)S(1)}, bf16[4,3,22,800]{3,2,1,0:T(8,128)(2,1)S(1)}, u32[]{:S(2)}, u32[]{:S(2)}) collective-permute-start(bf16[4,3,22,800]{3,2,1,0:T(8,128)(2,1)S(1)} %get-tuple-element.460), channel_id=1, source_target_pairs={{8,0},{16,8},{24,16},{9,1},{17,9},{25,17},{10,2},{18,10},{26,18},{... | collective-permute-start | bytes 1267208 | tf_op jit(solution)/shard_map/ppermute | solution.py:20
  383.7 8.3 collective-permute-start.8
  383.8 8.3 collective-permute-start.9
  392.6 15.1 collective-permute-start.10
  396.8 23.6 %collective-permute-start.11 = (bf16[4,3,38,400]{3,2,1,0:T(8,128)(2,1)S(1)}, bf16[4,3,38,400]{3,2,1,0:T(8,128)(2,1)}, u32[]{:S(2)}, u32[]{:S(2)}) collective-permute-start(bf16[4,3,38,400]{3,2,1,0:T(8,128)(2,1)S(1)} %get-tuple-element.439), channel_id=1, source_target_pairs={{8,0},{16,8},{24,16},{9,1},{17,9},{25,17},{10,2},{18,10},{26,18},{... | collective-permute-start | bytes 1094408 | tf_op jit(solution)/shard_map/ppermute | solution.py:20
  626.7 41.5 %collective-permute-start.12 = (bf16[4,12,3,400]{3,2,1,0:T(4,128)(2,1)}, bf16[4,12,3,400]{3,2,1,0:T(4,128)(2,1)S(1)}, u32[]{:S(2)}, u32[]{:S(2)}) collective-permute-start(bf16[4,12,3,400]{3,2,1,0:T(4,128)(2,1)} %get-tuple-element.447), channel_id=1, source_target_pairs={{0,1},{1,2},{2,3},{3,4},{4,5},{5,6},{6,7},{7,0},{8,9},{9,10},{10,1... | collective-permute-start | bytes 345608 | tf_op jit(solution)/shard_map/ppermute | solution.py:17
  626.7 41.5 %collective-permute-start.13 = (bf16[4,12,3,400]{3,2,1,0:T(4,128)(2,1)}, bf16[4,12,3,400]{3,2,1,0:T(4,128)(2,1)}, u32[]{:S(2)}, u32[]{:S(2)}) collective-permute-start(bf16[4,12,3,400]{3,2,1,0:T(4,128)(2,1)} %get-tuple-element.448), channel_id=1, source_target_pairs={{1,0},{2,1},{3,2},{4,3},{5,4},{6,5},{7,6},{0,7},{9,8},{10,9},{11,1... | collective-permute-start | bytes 345608 | tf_op jit(solution)/shard_map/ppermute | solution.py:20
  670.1 11.8 collective-permute-start.14
  674.3 20.2 collective-permute-start.15
  828.1 9.8 collective-permute-start.16
  828.1 9.8 collective-permute-start.17
  839.5 39.3 %collective-permute-start.18 = (bf16[4,3,22,800]{3,2,1,0:T(8,128)(2,1)}, bf16[4,3,22,800]{3,2,1,0:T(8,128)(2,1)S(1)}, u32[]{:S(2)}, u32[]{:S(2)}) collective-permute-start(bf16[4,3,22,800]{3,2,1,0:T(8,128)(2,1)} %get-tuple-element.455), channel_id=1, source_target_pairs={{0,8},{8,16},{16,24},{1,9},{9,17},{17,25},{2,10},{10,18},{18,26},{... | collective-permute-start | bytes 1267208 | tf_op jit(solution)/shard_map/ppermute | solution.py:17
  843.8 35.1 %collective-permute-start.19 = (bf16[4,3,22,800]{3,2,1,0:T(8,128)(2,1)}, bf16[4,3,22,800]{3,2,1,0:T(8,128)(2,1)}, u32[]{:S(2)}, u32[]{:S(2)}) collective-permute-start(bf16[4,3,22,800]{3,2,1,0:T(8,128)(2,1)} %get-tuple-element.456), channel_id=1, source_target_pairs={{8,0},{16,8},{24,16},{9,1},{17,9},{25,17},{10,2},{18,10},{26,18},{... | collective-permute-start | bytes 1267208 | tf_op jit(solution)/shard_map/ppermute | solution.py:20
  1790.6 417.0 %all-reduce.14.cloned.1.call-start = ((), (), s32[]{:S(2)}) async-start(), calls=%async_computation.5 | async-start | bytes 33923072
  1808.6 9.2 collective-permute-start.20
  1808.7 9.2 collective-permute-start.21
  1818.4 110.0 %collective-permute-start.22 = (bf16[4,3,38,400]{3,2,1,0:T(8,128)(2,1)S(1)}, bf16[4,3,38,400]{3,2,1,0:T(8,128)(2,1)}, u32[]{:S(2)}, u32[]{:S(2)}) collective-permute-start(bf16[4,3,38,400]{3,2,1,0:T(8,128)(2,1)S(1)} %get-tuple-element.430), channel_id=1, source_target_pairs={{0,8},{8,16},{16,24},{1,9},{9,17},{17,25},{2,10},{10,18},{18,26},{... | collective-permute-start | bytes 1094408 | tf_op jit(solution)/shard_map/ppermute | solution.py:17
  1822.8 105.6 %collective-permute-start.23 = (bf16[4,3,38,400]{3,2,1,0:T(8,128)(2,1)S(1)}, bf16[4,3,38,400]{3,2,1,0:T(8,128)(2,1)}, u32[]{:S(2)}, u32[]{:S(2)}) collective-permute-start(bf16[4,3,38,400]{3,2,1,0:T(8,128)(2,1)S(1)} %get-tuple-element.431), channel_id=1, source_target_pairs={{8,0},{16,8},{24,16},{9,1},{17,9},{25,17},{10,2},{18,10},{26,18},{... | collective-permute-start | bytes 1094408 | tf_op jit(solution)/shard_map/ppermute | solution.py:20
  (341 other events, 7701.7 us)
Sparse Core Ops, SparseCore 0:
  9.9 34.9 all-gather.18
  46.7 43.4 all-gather.10
  92.1 60.4 all-gather.12
  154.3 66.2 all-gather.14
  222.3 29.3 all-gather.20
  253.4 41.3 all-gather.16
  1790.8 127.8 all-reduce.11
  1926.0 281.6 all-reduce.13
where the time goes:
time: 2330 us; the launch traced here: 2300 us
  blocking collectives  791 us (34%)
  local copies, waits for them, and re-layouts  543 us (23%)
  waiting for transfers between devices  415 us (18%)
  other arithmetic  286 us (12%)
  matrix products  192 us (8%)
  starting transfers between devices  54.6 us (2%)
    unnamed x1, blocking collectives  554 us
    unnamed x720, local copies, waits for them, and re-layouts  288 us
    unnamed x9, waiting for transfers between devices  253 us
    psum x3, blocking collectives, block_forward(): lax.psum((local_sums[0], local_sums[1], local_sums[2]), ('lat', 'lon'))  121 us
    psum x1, waiting for transfers between devices, shards(): small_total = lax.psum(small_vector, ('lat', 'lon'))  94.5 us
    reduce_sum x11, other arithmetic, kernel_terms(): row_terms.append(jnp.sum(window * upstream, axis=(0, 1, 2)))  88.1 us
    psum x2, blocking collectives, block_backward(): lax.psum((local_back[0], local_back[1]), ('lat', 'lon'))  80.2 us
    dot_general x3, matrix products, block_forward(): jnp.dot(normed, up_weight, preferred_element_type=jnp.float32)  76 us
  transfers between devices with their start and end apart: 32, of which 10 were waited for; matrix products, arithmetic and copies ran while one was open for 18% of the time, Pallas kernels for 0%

commit v1 on v0

--- a/solution.py
+++ b/solution.py
@@ -118,7 +118,7 @@
         jnp.sum(grad_normed, axis=(0, 1, 2)),
         jnp.sum(grad_normed * unit_norm, axis=(0, 1, 2)),
     )
-    grad_shift, grad_gain = lax.psum((local_back[0], local_back[1]), ("lat", "lon"))
+    grad_shift, grad_gain = lax.psum(lax.psum((local_back[0], local_back[1]), "lon"), "lat")
     gain_float = scale_gain.astype(jnp.float32)
     grad_mixed = norm_factor * (
         gain_float * grad_normed

time: 2330 us -> 2200 us (0.944)
  waiting for transfers between devices: 415 us -> 301 us
    psum x1, waiting for transfers between devices: 94.5 us -> 0.02 us  [shards(): small_total = lax.psum(small_vector, ('lat', 'lon'))]
    unnamed x9, waiting for transfers between devices: 253 us -> 209 us
    ppermute x12, waiting for transfers between devices: 43.3 us -> 67.2 us  [padded(): lax.ppermute(lax.slice_in_dim(block, 0, width, axis=dim), axis, backward)]
    psum x2 -> x6, blocking collectives: 80.2 us -> 68.5 us  [the longest x3 41.4 us: block_backward(): lax.psum((local_back[0], local_back[1]), 'lon')]
    unnamed x720 -> x756, local copies, waits for them, and re-layouts: 288 us -> 287 us
  transfers between devices with their start and end apart: 32 -> 32, of which waited for: 10 -> 14; matrix products, arithmetic and copies ran while one was open for 18% -> 32% of each run, Pallas kernels for 0% -> 0%
where the time goes in v1:
time: 2200 us; the launch traced here: 2170 us
  blocking collectives  776 us (35%)
  local copies, waits for them, and re-layouts  547 us (25%)
  waiting for transfers between devices  301 us (14%)
  other arithmetic  288 us (13%)
  matrix products  196 us (9%)
  starting transfers between devices  42.3 us (2%)
    unnamed x1, blocking collectives  550 us
    unnamed x756, local copies, waits for them, and re-layouts  287 us
    unnamed x9, waiting for transfers between devices  209 us
    psum x3, blocking collectives, block_forward(): lax.psum((local_sums[0], local_sums[1], local_sums[2]), ('lat', 'lon'))  126 us
    reduce_sum x11, other arithmetic, kernel_terms(): row_terms.append(jnp.sum(window * upstream, axis=(0, 1, 2)))  90.4 us
    dot_general x3, matrix products, block_forward(): jnp.dot(normed, up_weight, preferred_element_type=jnp.float32)  76 us
    slice x18, local copies, waits for them, and re-layouts, unpack(): pieces.append(vector[offset:offset + length].reshape(extent))  71.3 us
    ppermute x12, waiting for transfers between devices, padded(): lax.ppermute(lax.slice_in_dim(block, 0, width, axis=dim), axis, backward)  67.2 us
  transfers between devices with their start and end apart: 32, of which 14 were waited for; matrix products, arithmetic and copies ran while one was open for 32% of the time, Pallas kernels for 0%

profile of v1, /device:TPU:0, one launch (start us, length us, event | category | flops | bytes accessed | tf_op | source)
XLA Modules:
  0.0 2171.9 jit_solution(7235238373120811850)
XLA Ops:
  35.9 17.0 all-gather.1
  55.0 14.5 all-gather.2
  124.2 25.7 %multiply_reduce_fusion.1 = (f32[400]{0:T(512)}, f32[400]{0:T(512)}, f32[4,12,32,400]{3,2,1,0:T(8,128)}) fusion(f32[4,12,32]{2,1,0:T(8,128)S(1)} %copy-done.49, bf16[4,15,38,400]{3,2,1,0:T(8,128)(2,1)S(1)} %get-tuple-element.446, f32[400]{0:T(512)S(1)} %bitcast.485, f32[400]{0:T(512)S(1)} %bitcast.484, f32[400]{0:T(512)S(1)} %bitcast.483, ...), kind=kLoop, calls=%fused_computation.214 | loop fusion | flops 97688800 | bytes 59185344 | tf_op jit(solution)/shard_map/reduce_sum | solution.py:77
  149.9 46.0 %all-reduce.4 = (f32[400]{0:T(512)S(1)}, f32[]{:T(128)}, f32[400]{0:T(512)S(1)}) all-reduce(f32[400]{0:T(512)} %get-tuple-element.207, f32[]{:T(128)} %convert_reduce_fusion.9, f32[400]{0:T(512)} %get-tuple-element.206), channel_id=1, replica_groups=mesh['lat'=4,'lon'=8] {'lat','lon'}, use_global_device_ids=true, to_apply=%region_5.0 | all-reduce | flops 801 | bytes 6408 | tf_op jit(solution)/shard_map/psum | solution.py:81
  202.1 29.4 %multiply_convert_fusion.1 = (bf16[1536,1600]{0,1:T(8,128)(2,1)}, f32[1536,1600]{0,1:T(8,128)}, f32[1536,1600]{0,1:T(8,128)}) fusion(f32[1600]{0:T(1024)S(1)} %copy-done.335, bf16[1536,400]{1,0:T(8,128)(2,1)S(1)} %bitcast.461, bf16[400,1600]{1,0:T(8,128)(2,1)} %reshape.643), kind=kOutput, calls=%fused_computation.171 | convolution fusion | flops 2128281600 | bytes 27091200 | tf_op jit(solution)/shard_map/dot_general | solution.py:92
  270.8 14.0 collective-permute-done.6
  284.8 12.9 collective-permute-done.7
  311.1 39.8 %all-reduce.3 = (f32[800]{0:T(1024)S(1)}, f32[]{:T(128)}, f32[800]{0:T(1024)S(1)}) all-reduce(f32[800]{0:T(1024)S(1)} %get-tuple-element.279, f32[]{:T(128)} %reduce_sum.1550, f32[800]{0:T(1024)S(1)} %get-tuple-element.278), channel_id=1, replica_groups=mesh['lat'=4,'lon'=8] {'lat','lon'}, use_global_device_ids=true, to_apply=%region_13.0 | all-reduce | flops 1601 | bytes 12808 | tf_op jit(solution)/shard_map/psum | solution.py:81
  351.9 16.4 multiply_convert_fusion.2
  404.9 12.4 collective-permute-done.11
  421.9 24.7 %multiply_reduce_fusion = (f32[400]{0:T(512)S(1)}, f32[400]{0:T(512)S(1)}, f32[4,12,32,400]{3,2,1,0:T(8,128)}) fusion(f32[4,12,32]{2,1,0:T(8,128)S(1)} %copy-done.51, bf16[4,15,38,400]{3,2,1,0:T(8,128)(2,1)S(1)} %get-tuple-element.442, f32[400]{0:T(512)S(1)} %bitcast.594, f32[400]{0:T(512)S(1)} %bitcast.593, f32[400]{0:T(512)S(1)} %bitcast.592, ...), kind=kLoop, calls=%fused_computation.212 | loop fusion | flops 103218400 | bytes 55614144 | tf_op jit(solution)/shard_map/reduce_sum | solution.py:77
  446.7 39.8 %all-reduce.2 = (f32[400]{0:T(512)S(1)}, f32[400]{0:T(512)S(1)}) all-reduce(f32[400]{0:T(512)S(1)} %get-tuple-element.205, f32[400]{0:T(512)S(1)} %get-tuple-element.204), channel_id=1, replica_groups=mesh['lat'=4,'lon'=8] {'lat','lon'}, use_global_device_ids=true, to_apply=%region_17.0 | all-reduce | flops 800 | bytes 6400 | tf_op jit(solution)/shard_map/psum | solution.py:81
  490.9 30.1 %multiply_convert_fusion = (bf16[1536,1600]{0,1:T(8,128)(2,1)}, f32[1536,1600]{0,1:T(8,128)}, f32[1536,1600]{0,1:T(8,128)}) fusion(f32[1600]{0:T(1024)S(1)} %copy-done.334, bf16[1536,400]{1,0:T(8,128)(2,1)S(1)} %bitcast.463, bf16[400,1600]{1,0:T(8,128)(2,1)S(1)} %copy-done.60), kind=kOutput, calls=%fused_computation.158 | convolution fusion | flops 2128281600 | bytes 27091200 | tf_op jit(solution)/shard_map/dot_general | solution.py:92
  544.0 13.9 all-reduce.7
  568.5 22.6 %fusion.193 = (f32[400]{0:T(512)S(1)}, f32[400]{0:T(512)S(1)}, f32[400]{0:T(512)S(1)}, f32[400]{0:T(512)S(1)}, f32[400]{0:T(512)S(1)}, /*index=5*/f32[400]{0:T(5...) fusion(bf16[4,15,38,400]{3,2,1,0:T(8,128)(2,1)} %copy-done.4, ...), kind=kLoop, calls=%fused_computation.486 | loop fusion | flops 39314400 | bytes 28305344 | tf_op jit(solution)/shard_map/reduce_sum | solution.py:50
  615.8 13.8 fusion.192
  665.0 25.0 %convert_reduce_fusion.4 = (f32[400]{0:T(512)}, bf16[4,12,32,400]{3,2,1,0:T(8,128)(2,1)S(1)}) fusion(bf16[4,15,38,400]{3,2,1,0:T(8,128)(2,1)S(1)} %get-tuple-element.438, f32[400]{0:T(512)} %bitcast.643, f32[400]{0:T(512)} %bitcast.642, f32[400]{0:T(512)} %bitcast.641, f32[400]{0:T(512)} %bitcast.640, f32[400]{0:T(512)} %bitcast.639, f32[400]{0:T(512)} %bitcast.638, ...), kind=kLoop, calls=%fused_computation.567 | loop fusion | flops 104447600 | bytes 55612544 | tf_op jit(solution)/shard_map/reduce_sum | solution.py:270
  718.8 13.9 all-reduce.6
  805.4 14.1 reshape.631
  837.2 12.8 collective-permute-done.19
  875.4 12.6 convert_reduce_fusion.1
  909.9 13.6 all-reduce.5
  995.3 87.2 %dynamic-update-slice.4 = f32[8480000]{0:T(1024)} dynamic-update-slice(f32[8480000]{0:T(1024)} %dynamic-update-slice.3, f32[2560000]{0:T(1024)} %reshape.630, s32[]{} %constant.210) | dynamic-update-slice | bytes 20480004
  1082.5 87.0 %dynamic-update-slice.5 = f32[8480000]{0:T(1024)} dynamic-update-slice(f32[8480000]{0:T(1024)} %dynamic-update-slice.4, f32[2560000]{0:T(1024)} %reshape.631, s32[]{} %constant.211) | dynamic-update-slice | bytes 20480004
  1169.5 17.6 dynamic-update-slice.6
  1187.1 21.8 %dynamic-update-slice.7 = f32[8480000]{0:T(1024)} dynamic-update-slice(f32[8480000]{0:T(1024)} %dynamic-update-slice.6, f32[640000]{0:T(1024)S(1)} %copy-done.29, s32[]{} %constant.213) | dynamic-update-slice | bytes 5120004
  1208.8 22.7 %dynamic-update-slice.8 = f32[8480000]{0:T(1024)} dynamic-update-slice(f32[8480000]{0:T(1024)} %dynamic-update-slice.7, f32[640000]{0:T(1024)} %reshape.637, s32[]{} %constant.214) | dynamic-update-slice | bytes 5120004 | tf_op jit(solution)/shard_map/concatenate | solution.py:305
  1231.5 550.5 %all-reduce.18 = bf16[8480000]{0:T(1024)(128)(2,1)} all-reduce(f32[8480000]{0:T(1024)} %dynamic-update-slice.8), channel_id=2, replica_groups=mesh['lat'=4,'lon'=8] {'lat','lon'}, use_global_device_ids=true, to_apply=%region_193.0.clone | all-reduce | flops 8480000 | bytes 50880000
  1831.9 12.6 collective-permute-done.23
  1848.5 25.4 %fusion.269 = bf16[4,12,32,400]{3,2,1,0:T(8,128)(2,1)} fusion(f32[4,12,32,400]{3,0,2,1:T(4,128)S(1)} %bitcast.451, bf16[4,12,32,400]{3,2,1,0:T(8,128)(2,1)S(1)} %copy-done.17, bf16[4,12,3,400]{3,2,1,0:T(4,128)(2,1)S(1)} %collective-permute-done.21, bf16[4,12,3,400]{3,2,1,0:T(4,128)(2,1)S(1)} %collective-permute-done.20, ...), kind=kLoop, calls=%fused_computation.563 | loop fusion | flops 102604800 | bytes 56839744 | tf_op jit(solution)/shard_map/convert_element_type | solution.py:293
  1873.9 206.2 %all-reduce.17.cloned.1.call-done = bf16[8480000]{0:T(1024)(128)(2,1)} async-done(((bf16[8480000]{0:T(1024)(128)(2,1)}), bf16[8480000]{0:T(1024)(128)(2,1)}) %all-reduce.17.cloned.1.call-update) | async-done | bytes 16960016
  2121.1 13.7 slice.3016
  (1070 shorter events, 641.5 us)
Async XLA Ops:
  7.2 191.9 %all-gather.19.cloned.1.call-start = ((), (), s32[]{:S(2)}) async-start(), calls=%async_computation.6 | async-start | bytes 1730560 | tf_op jit(solution)/shard_map/all_gather | solution.py:189
  8.0 223.6 %all-gather.11.cloned.1.call-start = ((), (), s32[]{:S(2)}) async-start(), calls=%async_computation | async-start | bytes 2048000 | tf_op jit(solution)/shard_map/all_gather | solution.py:190
  8.7 343.1 %all-gather.13.cloned.1.call-start = ((), (), s32[]{:S(2)}) async-start(), calls=%async_computation.1 | async-start | bytes 6400000 | tf_op jit(solution)/shard_map/all_gather | solution.py:192
  9.4 358.9 %all-gather.15.cloned.1.call-start = ((), (), s32[]{:S(2)}) async-start(), calls=%async_computation.2 | async-start | bytes 7168000 | tf_op jit(solution)/shard_map/all_gather | solution.py:193
  10.0 388.9 %all-gather.21.cloned.1.call-start = ((), (), s32[]{:S(2)}) async-start(), calls=%async_computation.7 | async-start | bytes 1730560 | tf_op jit(solution)/shard_map/all_gather | solution.py:195
  10.6 510.4 %all-gather.17.cloned.1.call-start = ((), (), s32[]{:S(2)}) async-start(), calls=%async_computation.3 | async-start | bytes 2048000 | tf_op jit(solution)/shard_map/all_gather | solution.py:196
  11.6 58.0 %collective-permute-start.1 = (bf16[4,12,3,400]{3,2,1,0:T(4,128)(2,1)}, bf16[4,12,3,400]{3,2,1,0:T(4,128)(2,1)}, u32[]{:S(2)}, u32[]{:S(2)}) collective-permute-start(bf16[4,12,3,400]{3,2,1,0:T(4,128)(2,1)} %get-tuple-element.457), channel_id=1, source_target_pairs={{1,0},{2,1},{3,2},{4,3},{5,4},{6,5},{7,6},{0,7},{9,8},{10,9},{11,1... | collective-permute-start | bytes 345608 | tf_op jit(solution)/shard_map/ppermute | solution.py:20
  16.1 53.5 %collective-permute-start = (bf16[4,12,3,400]{3,2,1,0:T(4,128)(2,1)}, bf16[4,12,3,400]{3,2,1,0:T(4,128)(2,1)}, u32[]{:S(2)}, u32[]{:S(2)}) collective-permute-start(bf16[4,12,3,400]{3,2,1,0:T(4,128)(2,1)} %get-tuple-element.456), channel_id=1, source_target_pairs={{0,1},{1,2},{2,3},{3,4},{4,5},{5,6},{6,7},{7,0},{8,9},{9,10},{10,1... | collective-permute-start | bytes 345608 | tf_op jit(solution)/shard_map/ppermute | solution.py:17
  16.1 1801.8 %all-reduce.15.cloned.1.call-start = ((), (), s32[]{:S(2)}) async-start(), calls=%async_computation.4 | async-start | bytes 704512 | tf_op jit(solution)/shard_map/psum | solution.py:325
  71.9 47.6 %collective-permute-start.2 = (bf16[4,3,38,400]{3,2,1,0:T(8,128)(2,1)}, bf16[4,3,38,400]{3,2,1,0:T(8,128)(2,1)}, u32[]{:S(2)}, u32[]{:S(2)}) collective-permute-start(bf16[4,3,38,400]{3,2,1,0:T(8,128)(2,1)} %get-tuple-element.447), channel_id=1, source_target_pairs={{0,8},{8,16},{16,24},{1,9},{9,17},{17,25},{2,10},{10,18},{18,26},{... | collective-permute-start | bytes 1094408 | tf_op jit(solution)/shard_map/ppermute | solution.py:17
  74.9 44.6 %collective-permute-start.3 = (bf16[4,3,38,400]{3,2,1,0:T(8,128)(2,1)}, bf16[4,3,38,400]{3,2,1,0:T(8,128)(2,1)}, u32[]{:S(2)}, u32[]{:S(2)}) collective-permute-start(bf16[4,3,38,400]{3,2,1,0:T(8,128)(2,1)} %get-tuple-element.448), channel_id=1, source_target_pairs={{8,0},{16,8},{24,16},{9,1},{17,9},{25,17},{10,2},{18,10},{26,18},{... | collective-permute-start | bytes 1094408 | tf_op jit(solution)/shard_map/ppermute | solution.py:20
  254.3 5.9 collective-permute-start.5
  256.5 6.6 collective-permute-start.4
  264.2 20.6 collective-permute-start.6
  267.2 30.5 %collective-permute-start.7 = (bf16[4,3,22,800]{3,2,1,0:T(8,128)(2,1)S(1)}, bf16[4,3,22,800]{3,2,1,0:T(8,128)(2,1)S(1)}, u32[]{:S(2)}, u32[]{:S(2)}) collective-permute-start(bf16[4,3,22,800]{3,2,1,0:T(8,128)(2,1)S(1)} %get-tuple-element.465), channel_id=1, source_target_pairs={{8,0},{16,8},{24,16},{9,1},{17,9},{25,17},{10,2},{18,10},{26,18},{... | collective-permute-start | bytes 1267208 | tf_op jit(solution)/shard_map/ppermute | solution.py:20
  382.5 6.1 collective-permute-start.9
  383.6 7.8 collective-permute-start.8
  392.0 13.0 collective-permute-start.10
  396.9 20.4 collective-permute-start.11
  615.1 19.5 collective-permute-start.13
  615.1 19.5 collective-permute-start.12
  635.2 17.1 collective-permute-start.14
  637.7 23.3 %collective-permute-start.15 = (bf16[4,3,38,400]{3,2,1,0:T(8,128)(2,1)S(1)}, bf16[4,3,38,400]{3,2,1,0:T(8,128)(2,1)}, u32[]{:S(2)}, u32[]{:S(2)}) collective-permute-start(bf16[4,3,38,400]{3,2,1,0:T(8,128)(2,1)S(1)} %get-tuple-element.440), channel_id=1, source_target_pairs={{8,0},{16,8},{24,16},{9,1},{17,9},{25,17},{10,2},{18,10},{26,18},{... | collective-permute-start | bytes 1094408 | tf_op jit(solution)/shard_map/ppermute | solution.py:20
  767.8 51.7 %collective-permute-start.17 = (bf16[4,6,3,800]{3,2,1,0:T(4,128)(2,1)}, bf16[4,6,3,800]{3,2,1,0:T(4,128)(2,1)S(1)}, u32[]{:S(2)}, u32[]{:S(2)}) collective-permute-start(bf16[4,6,3,800]{3,2,1,0:T(4,128)(2,1)} %get-tuple-element.468), channel_id=1, source_target_pairs={{1,0},{2,1},{3,2},{4,3},{5,4},{6,5},{7,6},{0,7},{9,8},{10,9},{11,1... | collective-permute-start | bytes 345608 | tf_op jit(solution)/shard_map/ppermute | solution.py:20
  767.8 51.7 %collective-permute-start.16 = (bf16[4,6,3,800]{3,2,1,0:T(4,128)(2,1)}, bf16[4,6,3,800]{3,2,1,0:T(4,128)(2,1)}, u32[]{:S(2)}, u32[]{:S(2)}) collective-permute-start(bf16[4,6,3,800]{3,2,1,0:T(4,128)(2,1)} %get-tuple-element.467), channel_id=1, source_target_pairs={{0,1},{1,2},{2,3},{3,4},{4,5},{5,6},{6,7},{7,0},{8,9},{9,10},{10,1... | collective-permute-start | bytes 345608 | tf_op jit(solution)/shard_map/ppermute | solution.py:17
  822.1 15.0 collective-permute-start.18
  826.2 23.8 %collective-permute-start.19 = (bf16[4,3,22,800]{3,2,1,0:T(8,128)(2,1)}, bf16[4,3,22,800]{3,2,1,0:T(8,128)(2,1)}, u32[]{:S(2)}, u32[]{:S(2)}) collective-permute-start(bf16[4,3,22,800]{3,2,1,0:T(8,128)(2,1)} %get-tuple-element.461), channel_id=1, source_target_pairs={{8,0},{16,8},{24,16},{9,1},{17,9},{25,17},{10,2},{18,10},{26,18},{... | collective-permute-start | bytes 1267208 | tf_op jit(solution)/shard_map/ppermute | solution.py:20
  969.5 1110.7 %all-reduce.17.cloned.1.call-start = ((), (), s32[]{:S(2)}) async-start(), calls=%async_computation.5 | async-start | bytes 33923072
  1799.9 8.5 collective-permute-start.21
  1800.7 8.8 collective-permute-start.20
  1810.0 21.9 %collective-permute-start.22 = (bf16[4,3,38,400]{3,2,1,0:T(8,128)(2,1)S(1)}, bf16[4,3,38,400]{3,2,1,0:T(8,128)(2,1)}, u32[]{:S(2)}, u32[]{:S(2)}) collective-permute-start(bf16[4,3,38,400]{3,2,1,0:T(8,128)(2,1)S(1)} %get-tuple-element.435), channel_id=1, source_target_pairs={{0,8},{8,16},{16,24},{1,9},{9,17},{17,25},{2,10},{10,18},{18,26},{... | collective-permute-start | bytes 1094408 | tf_op jit(solution)/shard_map/ppermute | solution.py:17
  1816.6 27.9 %collective-permute-start.23 = (bf16[4,3,38,400]{3,2,1,0:T(8,128)(2,1)S(1)}, bf16[4,3,38,400]{3,2,1,0:T(8,128)(2,1)}, u32[]{:S(2)}, u32[]{:S(2)}) collective-permute-start(bf16[4,3,38,400]{3,2,1,0:T(8,128)(2,1)S(1)} %get-tuple-element.436), channel_id=1, source_target_pairs={{8,0},{16,8},{24,16},{9,1},{17,9},{25,17},{10,2},{18,10},{26,18},{... | collective-permute-start | bytes 1094408 | tf_op jit(solution)/shard_map/ppermute | solution.py:20
  (359 other events, 5896.1 us)
Sparse Core Ops, SparseCore 0:
  9.9 32.2 all-gather.18
  44.0 35.4 all-gather.10
  81.3 66.9 all-gather.12
  150.0 66.4 all-gather.14
  218.2 29.4 all-gather.20
  249.4 40.3 all-gather.16
  969.6 123.7 all-reduce.14
  1798.5 281.6 all-reduce.16
